TPU v7x, 128 devices: a whole 4x4x4 slice. The times are simulated.
128 devices in a mesh: row: 8 (over y, z_hi), col: 16 (over x, z_lo, core).
Axes of the slice: x: 4, y: 4, z: 4 (z_hi: 2, z_lo: 2; z = z_hi * 2 + z_lo), core: 2. Of those that a mesh axis runs over, the one named last changes fastest.
Arguments:
- band_factors: bfloat16 [48, 48, 8, 256], P('col'), may hold values from -6 to 6
- pair_density: bfloat16 [48, 48, 16, 256], P('col'), may hold values from -6 to 6
- screened: bfloat16 [48, 48, 256, 256], P('col'), may hold values from -1 to 3, as said below
- coulomb: float32 [256], replicated, may hold values from 0.2 to 2
- window_mask: int32 [3, 48, 48], P(None, 'row'), may hold values 0 or 1
- trial_vector: bfloat16 [16, 48, 48], P(None, 'col'), may hold values from -0.0013809204 to 0.0013809204
Outputs:
- row_image: float32 [16, 3, 48], P('col', None, 'row')
- col_image: float32 [16, 48, 48], P(None, 'col', 'row')
Inputs may be any that keep to these rules, and one draw needn't show every extreme that they name: `screened`: every block is symmetric.
All inputs are finite; a program needn't handle non-finite values. No bound on the sum of `window_mask` on one device may be relied on, other than what follows from the above.
Results may differ from a plain program's by a relative error of at most 0.0041.
Values may be sent and summed in bfloat16 or wider, within the bound.
A program may use at most 192 MiB of HBM per device.

v0:
```python
import jax
import jax.numpy as jnp
from jax import lax
from jax.sharding import PartitionSpec as P

HIGHEST_PRECISION = lax.Precision.HIGHEST


def broadcast(block, axis, holder):
    block = jnp.where(lax.axis_index(axis) == holder, block, jnp.zeros_like(block))
    return lax.psum(block, axis)


def shifted(block, axis, distance):
    devices = range(lax.axis_size(axis))
    route = [(i - distance, i) for i in devices if i - distance in devices]
    return lax.ppermute(block, axis, route)


def slab_terms(
    row_bands,
    row_pairs,
    row_trial,
    row_lines,
    first_b,
    col_bands,
    col_pairs,
    col_trial,
    col_lines,
    blocks,
    q_values,
    kept_mask,
    coulomb,
):
    line_count, row_width = (row_bands.shape[0], row_bands.shape[1])
    mesh_side = col_bands.shape[1]
    band_half = row_bands.shape[2] // 2
    fourier = row_bands.shape[3]
    q_count = q_values.shape[0]
    within = jnp.arange(row_width, dtype=jnp.int32)
    places = (first_b + within[None, :] + q_values[:, None]) % mesh_side
    chosen_bands = jnp.take(col_bands, places, axis=1)
    chosen_pairs = jnp.take(col_pairs, places, axis=1)
    left_pair = (
        row_bands[:, None, :, :band_half, None, :] * chosen_bands[:, :, :, None, :band_half, :]
    )
    right_pair = (
        row_bands[:, None, :, band_half:, None, :] * chosen_bands[:, :, :, None, band_half:, :]
    )
    mixed_pair = jnp.einsum(
        "tqmg,qgh->tqmh",
        left_pair.reshape(line_count, q_count, row_width * band_half * band_half, fourier),
        blocks,
        preferred_element_type=jnp.float32,
    ).astype(jnp.bfloat16)
    mixed_pair = mixed_pair.reshape(line_count, q_count, row_width, band_half, band_half, fourier)
    direct = jnp.einsum(
        "tqiach,tqivwh->tqivawc", mixed_pair, right_pair, preferred_element_type=jnp.float32
    )
    direct = direct.reshape(
        line_count, q_count, row_width, band_half * band_half, band_half * band_half
    )
    scaled = (row_pairs.astype(jnp.float32) * coulomb).astype(jnp.bfloat16)
    exchange_term = jnp.einsum(
        "tisg,tqiug->tqisu", scaled, chosen_pairs, preferred_element_type=jnp.float32
    )
    kernel = 2.0 * exchange_term - direct
    row_place = row_lines[:, None] * mesh_side + first_b + within[None, :]
    col_place = col_lines[:, None, None] * mesh_side + places[None, :, :]
    kept = (col_place >= row_place[:, None, :]) & (kept_mask[:, None, :] > 0)
    kernel = jnp.where(kept[..., None, None], kernel, 0.0)
    chosen_trial = jnp.take(col_trial, places, axis=2)
    row_part = jnp.einsum("tqisu,utqi->sti", kernel, chosen_trial, precision=HIGHEST_PRECISION)
    strict = col_place > row_place[:, None, :]
    col_each = jnp.einsum(
        "tqisu,sti->utqi",
        jnp.where(strict[..., None, None], kernel, 0.0),
        row_trial,
        precision=HIGHEST_PRECISION,
    )
    onehot = (places[:, :, None] == jnp.arange(mesh_side, dtype=jnp.int32)[None, None, :]).astype(
        jnp.float32
    )
    col_part = jnp.einsum("utqi,qic->utc", col_each, onehot, precision=HIGHEST_PRECISION)
    return (row_part, col_part)


def add_into(total, part, start):
    piece = lax.dynamic_slice_in_dim(total, start, part.shape[1], 1)
    return lax.dynamic_update_slice_in_dim(total, piece + part, start, 1)


def local(band_factors, pair_density, screened, coulomb, window_mask, trial_vector):
    col_count = lax.axis_size("col")
    col_index = lax.axis_index("col")
    row_index = lax.axis_index("row")
    midway = col_count // 2
    band_lines, mesh_side = (band_factors.shape[0], band_factors.shape[1])
    row_width = window_mask.shape[1]
    first_b = row_index * row_width
    picked = (
        lax.dynamic_slice_in_dim(band_factors, first_b, row_width, 1),
        lax.dynamic_slice_in_dim(pair_density, first_b, row_width, 1),
        lax.dynamic_slice_in_dim(trial_vector, first_b, row_width, 2),
    )
    row_bands, row_pairs, row_trial = (
        broadcast(picked[0], "col", midway),
        broadcast(picked[1], "col", midway),
        broadcast(picked[2], "col", midway),
    )
    row_trial = row_trial.astype(jnp.float32)
    panel_first = band_lines * midway
    all_q = jnp.arange(mesh_side, dtype=jnp.int32)

    def compute_slab(
        row_start,
        col_start,
        line_count,
        col_band_first,
        col_bands,
        col_pairs,
        col_trial,
        blocks,
        q_values,
    ):
        row_lines = panel_first + row_start + jnp.arange(line_count, dtype=jnp.int32)
        col_lines = col_band_first + col_start + jnp.arange(line_count, dtype=jnp.int32)
        mask_rows = lax.dynamic_slice_in_dim(window_mask, row_start, line_count, 0)
        line_index = jnp.broadcast_to(
            (col_lines % mesh_side)[:, None, None], (line_count, row_width, 1)
        )
        kept_mask = jnp.take_along_axis(mask_rows, line_index, axis=2)[:, :, 0]
        return slab_terms(
            lax.dynamic_slice_in_dim(row_bands, row_start, line_count, 0),
            lax.dynamic_slice_in_dim(row_pairs, row_start, line_count, 0),
            lax.dynamic_slice_in_dim(row_trial, row_start, line_count, 1),
            row_lines,
            first_b,
            lax.dynamic_slice_in_dim(col_bands, col_start, line_count, 0),
            lax.dynamic_slice_in_dim(col_pairs, col_start, line_count, 0),
            lax.dynamic_slice_in_dim(col_trial, col_start, line_count, 1),
            col_lines,
            blocks,
            q_values,
            kept_mask,
            coulomb,
        )

    is_live = col_index >= midway
    live_flag = is_live.astype(jnp.int32)
    received = shifted((band_factors, pair_density, trial_vector), "col", -midway)
    col_bands = jnp.where(is_live, band_factors, received[0])
    col_pairs = jnp.where(is_live, pair_density, received[1])
    col_trial = jnp.where(is_live, trial_vector, received[2]).astype(jnp.float32)
    col_band_first = jnp.where(is_live, col_index, col_index + midway) * band_lines
    center = shifted(screened[0, mesh_side // 2 :], "col", midway)
    blocks = jnp.where(is_live, center, screened[0, : mesh_side // 2])
    q_values = all_q[: mesh_side // 2] + live_flag * (mesh_side // 2)
    row_part, col_part = compute_slab(
        0, 0, band_lines, col_band_first, col_bands, col_pairs, col_trial, blocks, q_values
    )
    row_total = row_part
    col_total = col_part
    below_rows = shifted(screened[1:], "col", midway + 1)
    for line_gap in range(1, band_lines):
        blocks = jnp.where(is_live, below_rows[band_lines - 1 - line_gap], screened[line_gap])
        row_start = live_flag * line_gap
        col_start = (1 - live_flag) * line_gap
        row_part, col_part = compute_slab(
            row_start,
            col_start,
            band_lines - line_gap,
            col_band_first,
            col_bands,
            col_pairs,
            col_trial,
            blocks,
            all_q,
        )
        row_total = add_into(row_total, row_part, row_start)
        col_total = add_into(col_total, col_part, col_start)
    returned = shifted(col_total, "col", midway)
    col_total = jnp.where(is_live, col_total + returned, 0.0)
    row_image = lax.psum_scatter(row_total, "col", scatter_dimension=0, tiled=True)
    col_image = lax.psum_scatter(col_total, "row", scatter_dimension=2, tiled=True)
    return (row_image, col_image)


def solution(mesh):
    placed = (
        P("col", None, None, None),
        P("col", None, None, None),
        P("col", None, None, None),
        P(),
        P(None, "row", None),
        P(None, "col", None),
    )
    return jax.shard_map(
        local,
        mesh=mesh,
        in_specs=placed,
        out_specs=(P("col", None, "row"), P(None, "col", "row")),
        check_vma=False,
    )
```

profile of v0, /device:TPU:0, one launch (start us, length us, event | category | flops | bytes accessed | tf_op | source)
XLA Modules:
  0.0 808.4 jit_solution(10363889306173101909)
XLA Ops:
  8.5 10.6 %slice.69 = bf16[2,48,256,256]{3,2,1,0:T(8,128)(2,1)} slice(bf16[3,48,256,256]{3,2,1,0:T(8,128)(2,1)} %param.8), slice={[1:3], [0:48], [0:256], [0:256]} | slice | bytes 25165824 | tf_op jit(solution)/shard_map/slice | solution.py:164
  19.1 9.2 %collective-permute-start.4 = (bf16[2,48,256,256]{3,2,1,0:T(8,128)(2,1)}, bf16[2,48,256,256]{3,2,1,0:T(8,128)(2,1)}, u32[]{:S(2)}, u32[]{:S(2)}) collective-permute-start(bf16[2,48,256,256]{3,2,1,0:T(8,128)(2,1)} %slice.69), channel_id=1, source_target_pairs={{0,9},{1,10},{2,11},{3,12},{4,13},{5,14},{6,15},{16,25},{17,26},{1... | collective-permute-start | bytes 37748744 | tf_op jit(solution)/shard_map/ppermute | solution.py:17
  34.8 8.9 %collective-permute-start.3 = (bf16[24,256,256]{2,1,0:T(8,128)(2,1)}, bf16[24,256,256]{2,1,0:T(8,128)(2,1)}, u32[]{:S(2)}, u32[]{:S(2)}) collective-permute-start(bf16[24,256,256]{2,1,0:T(8,128)(2,1)} %slice_bitcast_fusion), channel_id=1, source_target_pairs={{0,8},{1,9},{2,10},{3,11},{4,12},{5,13},{6,14},{7,15},{16,24},{17,... | collective-permute-start | bytes 9437192 | tf_op jit(solution)/shard_map/ppermute | solution.py:17
  49.7 332.8 %psum.23 = bf16[16,3,6]{0,2,1:T(8,128)(2,1)S(1)} all-reduce(bf16[16,3,6]{0,2,1:T(8,128)(2,1)S(1)} %broadcast_select_fusion.4), channel_id=1, replica_groups=mesh['row'=8,'col'=16] {'col'}, use_global_device_ids=true, to_apply=%region_3.4 | all-reduce | flops 288 | bytes 1152 | tf_op jit(solution)/shard_map/psum | solution.py:11
  396.3 35.1 %all-reduce.5.cloned.1.call-done = (bf16[3,6,8,256]{3,2,1,0:T(8,128)(2,1)}, bf16[3,6,16,256]{3,2,1,0:T(8,128)(2,1)}) async-done(((bf16[3,6,8,256]{3,2,1,0:T(8,128)(2,1)}, bf16[3,6,16,256]{3,2,1,0:T(8,128)(2,1)}), (bf16[3,6,8,256]{3,2,1,0:T(8,128)(2,1)}, bf16[3,6,16,256]{3,2,1,0:T(8,128)(2,1)})) %all-reduce.5.cloned.1.call-update) | async-done | bytes 221200 | tf_op jit(solution)/shard_map/psum | solution.py:11
  447.8 7.8 mul.255
  460.4 6.8 mul.239
  477.9 13.6 %gather_fusion.4 = bf16[288,2,16,256]{3,2,1,0:T(8,128)(2,1)} fusion(bf16[2,48,16,256]{3,2,1,0:T(8,128)(2,1)S(1)} %constant_dynamic-slice_fusion.8, s32[1024]{0:T(1024)S(1)} %pad_clamp_fusion), kind=kCustom, calls=%fused_computation.4 | custom fusion | bytes 9438336 | tf_op jit(solution)/shard_map/jit(_take)/gather | solution.py:43
  494.5 6.2 convert_bitcast_fusion.1
  500.7 5.7 reshape.941
  506.4 20.6 %convolution_bitcast_fusion.1 = f32[3,24,6,4,4,4,4]{6,5,4,3,2,1,0:T(4,128)} fusion(bf16[3,6,4,256]{3,2,1,0:T(4,128)(2,1)} %get-tuple-element.20, bf16[3,24,6,4,4,256]{5,4,3,2,0,1:T(4,128)(2,1)S(1)} %reshape.941, bf16[3,24,6,4,256]{4,3,0,2,1:T(4,128)(2,1)} %get-tuple-element.12), kind=kOutput, calls=%fused_computation.13 | convolution fusion | flops 63700992 | bytes 4902912 | tf_op jit(solution)/shard_map/tqiach,tqivwh->tqivawc/dot_general | solution.py:57
  526.9 13.2 %copy.66 = f32[3,24,6,4,4,4,4]{1,6,5,4,3,2,0:T(4,128)S(1)} copy(f32[3,24,6,4,4,4,4]{6,5,4,3,2,1,0:T(4,128)} %convolution_bitcast_fusion.1) | data formatting | bytes 884736 | tf_op jit(solution)/shard_map/tqiach,tqivwh->tqivawc/transpose | solution.py:57
  547.3 13.7 %fusion.23 = f32[3,6,1,24,16]{4,2,3,1,0:T(1,128)} fusion(f32[3,24,6,16,16]{3,4,1,2,0:T(8,128)S(1)} %fusion.20, pred[3,24,6]{1,2,0:T(8,128)(4,1)S(1)} %copy-done.23, bf16[16,3,6,1,1]{0,2,1,3,4:T(8,128)(2,1)S(1)} %bitcast.283), kind=kOutput, calls=%fused_computation.45 | convolution fusion | flops 1437696 | bytes 471024 | tf_op jit(solution)/shard_map/tqisu,sti->utqi/dot_general | solution.py:75
  567.0 9.1 %convert_bitcast_fusion = bf16[2,48,96,256]{3,2,0,1:T(8,128)(2,1)} fusion(bf16[2,48,96,256]{3,2,0,1:T(8,128)(2,1)} %mul.255, bf16[2,48,256,256]{3,2,1,0:T(8,128)(2,1)} %collective-permute-done.4, bf16[3,48,256,256]{3,2,1,0:T(8,128)(2,1)} %param.8, pred[]{:T(512)S(6)} %ge.124, bf16[2,96,256]{2,1,0:T(8,128)(2,1)S(1)} %copy-done.13), kind=kOutput, calls=%fused_computation.34 | convolution fusion | flops 1222901760 | bytes 22118400 | tf_op jit(solution)/shard_map/tqmg,qgh->tqmh/dot_general | solution.py:50
  576.1 7.8 reshape.943
  583.9 46.0 %convolution_bitcast_fusion = f32[2,48,6,4,4,4,4]{6,5,4,3,2,1,0:T(4,128)} fusion(bf16[2,6,4,256]{3,2,1,0:T(4,128)(2,1)S(1)} %copy-done.21, bf16[2,48,6,4,4,256]{5,4,3,2,0,1:T(4,128)(2,1)} %reshape.943, bf16[2,48,6,4,256]{4,3,0,2,1:T(4,128)(2,1)S(1)} %copy-done.5), kind=kOutput, calls=%fused_computation.12 | convolution fusion | flops 84934656 | bytes 6512640 | tf_op jit(solution)/shard_map/tqiach,tqivwh->tqivawc/dot_general | solution.py:57
  629.8 15.6 %copy.75 = f32[2,48,6,4,4,4,4]{1,6,5,4,3,2,0:T(4,128)S(1)} copy(f32[2,48,6,4,4,4,4]{6,5,4,3,2,1,0:T(4,128)} %convolution_bitcast_fusion) | data formatting | bytes 1179648 | tf_op jit(solution)/shard_map/tqiach,tqivwh->tqivawc/transpose | solution.py:57
  649.0 5.9 multiply_reduce_fusion.1
  657.4 8.2 %convert_bitcast_fusion.2 = bf16[1,48,96,256]{3,2,1,0:T(8,128)(2,1)} fusion(bf16[2,48,256,256]{3,2,1,0:T(8,128)(2,1)} %collective-permute-done.4, bf16[3,48,256,256]{3,2,1,0:T(8,128)(2,1)} %param.8, pred[]{:T(512)S(6)} %ge.124, bf16[48,96,256]{2,1,0:T(8,128)(2,1)S(1)} %copy-done.4, bf16[96,256]{1,0:T(8,128)(2,1)S(1)} %copy-done.16), kind=kOutput, calls=%fused_computation.69 | convolution fusion | flops 613023744 | bytes 17350656 | tf_op jit(solution)/shard_map/tqmg,qgh->tqmh/dot_general | solution.py:50
  669.8 12.8 %convolution_bitcast_fusion.2 = f32[1,48,6,4,4,4,4]{6,5,4,3,2,1,0:T(4,128)} fusion(bf16[48,6,4,4,256,1]{4,3,2,1,0,5:T(4,128)(2,1)S(1)} %reshape.1099, bf16[48,6,4,256]{3,2,1,0:T(4,128)(2,1)S(1)} %copy-done.8, bf16[6,4,256]{2,1,0:T(4,128)(2,1)S(1)} %copy-done.24), kind=kOutput, calls=%fused_computation.24 | convolution fusion | flops 42467328 | bytes 3256320 | tf_op jit(solution)/shard_map/tqiach,tqivwh->tqivawc/dot_general | solution.py:57
  682.6 8.2 %copy.82 = f32[1,48,6,4,4,4,4]{1,6,5,4,3,2,0:T(4,128)S(1)} copy(f32[1,48,6,4,4,4,4]{6,5,4,3,2,1,0:T(4,128)} %convolution_bitcast_fusion.2) | data formatting | bytes 589824 | tf_op jit(solution)/shard_map/tqiach,tqivwh->tqivawc/transpose | solution.py:57
  693.2 4.4 fusion.43
  700.9 55.7 %all-reduce = f32[16,3,6]{2,1,0:T(4,128)S(1)} all-reduce(f32[16,3,6]{2,1,0:T(4,128)S(1)} %copy.84), channel_id=2, replica_groups=mesh['row'=8,'col'=16] {'col'}, use_global_device_ids=true, to_apply=%region_2.3.clone | all-reduce | flops 288 | bytes 2304
  757.9 42.8 %all-reduce.1 = f32[16,3,48]{0,1,2:T(4,128)S(1)} all-reduce(f32[16,3,48]{0,1,2:T(4,128)S(1)} %copy.87), channel_id=3, replica_groups=mesh['row'=8,'col'=16] {'row'}, use_global_device_ids=true, to_apply=%region_4.5.clone | all-reduce | flops 2304 | bytes 18432
  (220 shorter events, 92.1 us)
Async XLA Ops:
  7.2 39.3 %copy-start = (s32[3,6,48]{2,1,0:T(8,128)S(1)}, s32[3,6,48]{2,1,0:T(8,128)}, u32[]{:S(2)}) copy-start(s32[3,6,48]{2,1,0:T(8,128)} %param.10) | copy-start | bytes 10372
  7.2 21.1 %copy-start.17 = (bf16[16,3,48]{2,0,1:T(8,128)(2,1)S(1)}, bf16[16,3,48]{2,0,1:T(8,128)(2,1)}, u32[]{:S(2)}) copy-start(bf16[16,3,48]{2,0,1:T(8,128)(2,1)} %param.11) | copy-start | bytes 13828
  7.2 424.3 %all-reduce.5.cloned.1.call-start = ((), (), s32[]{:S(2)}) async-start(), calls=%async_computation | async-start | bytes 442368 | tf_op jit(solution)/shard_map/psum | solution.py:11
  7.2 430.2 %collective-permute-start.2 = (bf16[3,48,8,256]{3,2,1,0:T(8,128)(2,1)}, bf16[3,48,8,256]{3,2,1,0:T(8,128)(2,1)S(1)}, u32[]{:S(2)}, u32[]{:S(2)}) collective-permute-start(bf16[3,48,8,256]{3,2,1,0:T(8,128)(2,1)} %param.6), channel_id=1, source_target_pairs={{8,0},{9,1},{10,2},{11,3},{12,4},{13,5},{14,6},{15,7},{24,16},{25,... | collective-permute-start | bytes 1769480 | tf_op jit(solution)/shard_map/ppermute | solution.py:17
  19.1 26.2 %copy-start.6 = (bf16[3,48,8,256]{3,2,1,0:T(8,128)(2,1)S(1)}, bf16[3,48,8,256]{3,2,1,0:T(8,128)(2,1)}, u32[]{:S(2)}) copy-start(bf16[3,48,8,256]{3,2,1,0:T(8,128)(2,1)} %param.6) | copy-start | bytes 1769476
  19.1 547.9 %collective-permute-start.4 = (bf16[2,48,256,256]{3,2,1,0:T(8,128)(2,1)}, bf16[2,48,256,256]{3,2,1,0:T(8,128)(2,1)}, u32[]{:S(2)}, u32[]{:S(2)}) collective-permute-start(bf16[2,48,256,256]{3,2,1,0:T(8,128)(2,1)} %slice.69), channel_id=1, source_target_pairs={{0,9},{1,10},{2,11},{3,12},{4,13},{5,14},{6,15},{16,25},{17,26},{1... | collective-permute-start | bytes 37748744 | tf_op jit(solution)/shard_map/ppermute | solution.py:17
  28.3 360.6 %collective-permute-start = (bf16[16,3,48]{2,0,1:T(8,128)(2,1)S(1)}, bf16[16,3,48]{2,0,1:T(8,128)(2,1)S(1)}, u32[]{:S(2)}, u32[]{:S(2)}) collective-permute-start(bf16[16,3,48]{2,0,1:T(8,128)(2,1)S(1)} %copy-done.17), channel_id=1, source_target_pairs={{8,0},{9,1},{10,2},{11,3},{12,4},{13,5},{14,6},{15,7},{24,16},{25,... | collective-permute-start | bytes 13832 | tf_op jit(solution)/shard_map/ppermute | solution.py:17
  29.6 444.0 %collective-permute-start.1 = (bf16[3,48,16,256]{3,2,1,0:T(8,128)(2,1)}, bf16[3,48,16,256]{3,2,1,0:T(8,128)(2,1)}, u32[]{:S(2)}, u32[]{:S(2)}) collective-permute-start(bf16[3,48,16,256]{3,2,1,0:T(8,128)(2,1)} %param.7), channel_id=1, source_target_pairs={{8,0},{9,1},{10,2},{11,3},{12,4},{13,5},{14,6},{15,7},{24,16},{25,... | collective-permute-start | bytes 3538952 | tf_op jit(solution)/shard_map/ppermute | solution.py:17
  34.8 352.2 %copy-start.35 = (u32[128]{0:T(128)S(1)}, u32[128]{0:T(128)}, u32[]{:S(2)}) copy-start(u32[128]{0:T(128)} %constant.311) | copy-start | bytes 1540
  34.8 352.8 %copy-start.34 = (u32[128]{0:T(128)S(1)}, u32[128]{0:T(128)}, u32[]{:S(2)}) copy-start(u32[128]{0:T(128)} %constant.307) | copy-start | bytes 1540
  34.8 459.6 %collective-permute-start.3 = (bf16[24,256,256]{2,1,0:T(8,128)(2,1)}, bf16[24,256,256]{2,1,0:T(8,128)(2,1)}, u32[]{:S(2)}, u32[]{:S(2)}) collective-permute-start(bf16[24,256,256]{2,1,0:T(8,128)(2,1)} %slice_bitcast_fusion), channel_id=1, source_target_pairs={{0,8},{1,9},{2,10},{3,11},{4,12},{5,13},{6,14},{7,15},{16,24},{17,... | collective-permute-start | bytes 9437192 | tf_op jit(solution)/shard_map/ppermute | solution.py:17
  49.0 344.9 %copy-start.18 = (s32[24,6]{0,1:T(8,128)}, s32[24,6]{0,1:T(8,128)S(1)}, u32[]{:S(2)}) copy-start(s32[24,6]{0,1:T(8,128)S(1)} %copy.60) | copy-start | bytes 1732
  384.9 9.0 %copy-start.27 = (pred[48,6]{0,1:T(8,128)(4,1)}, pred[48,6]{0,1:T(8,128)(4,1)S(1)}, u32[]{:S(2)}) copy-start(pred[48,6]{0,1:T(8,128)(4,1)S(1)} %get-tuple-element.30) | copy-start | bytes 868
  386.4 82.7 %copy-start.10 = (pred[48,6]{1,0:T(8,128)(4,1)}, pred[48,6]{1,0:T(8,128)(4,1)S(1)}, u32[]{:S(2)}) copy-start(pred[48,6]{1,0:T(8,128)(4,1)S(1)} %copy.68) | copy-start | bytes 868
  447.8 7.8 copy-start.2
  547.3 19.4 %copy-start.19 = (s32[24,6]{0,1:T(8,128)S(1)}, s32[24,6]{0,1:T(8,128)}, u32[]{:S(2)}) copy-start(s32[24,6]{0,1:T(8,128)} %copy-done.18) | copy-start | bytes 1732
  576.1 7.8 copy-start.5
  576.1 7.8 copy-start.21
  682.6 10.6 %copy-start.3 = (bf16[288,16,256]{2,1,0:T(8,128)(2,1)S(1)}, bf16[288,16,256]{2,1,0:T(8,128)(2,1)}, u32[]{:S(2)}) copy-start(bf16[288,16,256]{2,1,0:T(8,128)(2,1)} %gather_fusion.7) | copy-start | bytes 7077892
  682.6 10.6 %copy-start.11 = (pred[48,6]{1,0:T(8,128)(4,1)S(1)}, pred[48,6]{1,0:T(8,128)(4,1)}, u32[]{:S(2)}) copy-start(pred[48,6]{1,0:T(8,128)(4,1)} %copy-done.10) | copy-start | bytes 868
  682.6 10.6 %copy-start.12 = (f32[6,48,16]{2,1,0:T(8,128)S(1)}, f32[6,48,16]{2,1,0:T(8,128)}, u32[]{:S(2)}) copy-start(f32[6,48,16]{2,1,0:T(8,128)} %copy.144) | copy-start | bytes 55300
  682.6 10.6 %copy-start.31 = (pred[48,6]{0,1:T(8,128)(4,1)S(1)}, pred[48,6]{0,1:T(8,128)(4,1)}, u32[]{:S(2)}) copy-start(pred[48,6]{0,1:T(8,128)(4,1)} %get-tuple-element.29) | copy-start | bytes 868
  693.2 108.2 %copy-start.1 = (s32[3,6,48]{2,1,0:T(8,128)S(1)}, s32[3,6,48]{2,1,0:T(8,128)}, u32[]{:S(2)}) copy-start(s32[3,6,48]{2,1,0:T(8,128)} %param.10) | copy-start | bytes 10372
  699.4 58.4 %collective-permute-start.5 = (f32[16,3,48]{2,0,1:T(8,128)S(1)}, f32[16,3,48]{2,0,1:T(8,128)S(1)}, u32[]{:S(2)}, u32[]{:S(2)}) collective-permute-start(f32[16,3,48]{2,0,1:T(8,128)S(1)} %fusion.75), channel_id=1, source_target_pairs={{0,8},{1,9},{2,10},{3,11},{4,12},{5,13},{6,14},{7,15},{16,24},{17,... | collective-permute-start | bytes 27656 | tf_op jit(solution)/shard_map/ppermute | solution.py:17
  (19 other events, 73.9 us)
Sparse Core Ops, SparseCore 0:
  46.1 385.3 all-reduce.4
where the time goes:
time: 813 us; the launch traced here: 808 us
  blocking collectives  431 us (53%)
  local copies, waits for them, and re-layouts  153 us (19%)
  matrix products  136 us (17%)
  waiting for transfers between devices  35.2 us (4%)
  starting transfers between devices  23.3 us (3%)
  between operations  15.8 us (2%)
  other arithmetic  14 us (2%)
    psum x1, blocking collectives, broadcast(): return lax.psum(block, axis)  333 us
    unnamed x2, blocking collectives  98.5 us
    dot_general x3, matrix products, slab_terms(): jnp.einsum('tqiach,tqivwh->tqivawc', mixed_pair, right_pair, preferred_el...  79.3 us
    transpose x3, local copies, waits for them, and re-layouts, slab_terms(): jnp.einsum('tqiach,tqivwh->tqivawc', mixed_pair, right_pair, preferred_el...  37 us
    psum x1, waiting for transfers between devices, broadcast(): return lax.psum(block, axis)  35.1 us
    mul x12, local copies, waits for them, and re-layouts, slab_terms(): row_bands[:, None, :, :band_half, None, :]  24.9 us
    dot_general x3, matrix products, slab_terms(): jnp.einsum('tqmg,qgh->tqmh', left_pair.reshape(line_count, q_count, row_w...  23.5 us
    ppermute x6, starting transfers between devices, shifted(): return lax.ppermute(block, axis, route)  23.2 us
  transfers between devices with their start and end apart: 7, of which 1 were waited for; matrix products, arithmetic and copies ran while one was open for 21% of the time, Pallas kernels for 0%

commit v1 on v0

--- a/solution.py
+++ b/solution.py
@@ -8,7 +8,7 @@
 
 def broadcast(block, axis, holder):
     block = jnp.where(lax.axis_index(axis) == holder, block, jnp.zeros_like(block))
-    return lax.psum(block, axis)
+    return jnp.sum(lax.all_gather(block, axis), axis=0)
 
 
 def shifted(block, axis, distance):

time: 813 us -> 767 us (0.943)
  waiting for transfers between devices: 35.2 us -> 0.05 us
  matrix products: 136 us -> 124 us
    psum x1 -> x0, blocking collectives: 333 us -> none  [broadcast(): return lax.psum(block, axis)]
    all_gather x0 -> x1, blocking collectives: none -> 333 us  [broadcast(): return jnp.sum(lax.all_gather(block, axis), axis=0)]
    psum x1 -> x0, waiting for transfers between devices: 35.1 us -> none  [broadcast(): return lax.psum(block, axis)]
    dot_general x1 -> x0, matrix products: 13.7 us -> none  [slab_terms(): jnp.einsum('tqisu,sti->utqi', jnp.where(strict[..., None, None], kernel,...]
  transfers between devices with their start and end apart: 7 -> 8, of which waited for: 1 -> 0; matrix products, arithmetic and copies ran while one was open for 21% -> 21% of each run, Pallas kernels for 0% -> 0%
where the time goes in v1:
time: 767 us; the launch traced here: 762 us
  blocking collectives  430 us (56%)
  local copies, waits for them, and re-layouts  151 us (20%)
  matrix products  124 us (16%)
  starting transfers between devices  23.2 us (3%)
  other arithmetic  18.4 us (2%)
  between operations  15.8 us (2%)
    all_gather x1, blocking collectives, broadcast(): return jnp.sum(lax.all_gather(block, axis), axis=0)  333 us
    unnamed x2, blocking collectives  96.9 us
    dot_general x3, matrix products, slab_terms(): jnp.einsum('tqiach,tqivwh->tqivawc', mixed_pair, right_pair, preferred_el...  79.3 us
    transpose x3, local copies, waits for them, and re-layouts, slab_terms(): jnp.einsum('tqiach,tqivwh->tqivawc', mixed_pair, right_pair, preferred_el...  37 us
    mul x12, local copies, waits for them, and re-layouts, slab_terms(): row_bands[:, None, :, :band_half, None, :]  24.7 us
    dot_general x3, matrix products, slab_terms(): jnp.einsum('tqmg,qgh->tqmh', left_pair.reshape(line_count, q_count, row_w...  23.9 us
    ppermute x6, starting transfers between devices, shifted(): return lax.ppermute(block, axis, route)  23.1 us
    gather x3, local copies, waits for them, and re-layouts, slab_terms(): chosen_pairs = jnp.take(col_pairs, places, axis=1)  19.4 us
  transfers between devices with their start and end apart: 8, of which 0 were waited for; matrix products, arithmetic and copies ran while one was open for 21% of the time, Pallas kernels for 0%

profile of v1, /device:TPU:0, one launch (start us, length us, event | category | flops | bytes accessed | tf_op | source)
XLA Modules:
  0.0 762.1 jit_solution(2657715709119834051)
XLA Ops:
  10.2 10.6 %slice.69 = bf16[2,48,256,256]{3,2,1,0:T(8,128)(2,1)} slice(bf16[3,48,256,256]{3,2,1,0:T(8,128)(2,1)} %param.8), slice={[1:3], [0:48], [0:256], [0:256]} | slice | bytes 25165824 | tf_op jit(solution)/shard_map/slice | solution.py:164
  20.7 9.1 %collective-permute-start.4 = (bf16[2,48,256,256]{3,2,1,0:T(8,128)(2,1)}, bf16[2,48,256,256]{3,2,1,0:T(8,128)(2,1)}, u32[]{:S(2)}, u32[]{:S(2)}) collective-permute-start(bf16[2,48,256,256]{3,2,1,0:T(8,128)(2,1)} %slice.69), channel_id=1, source_target_pairs={{0,9},{1,10},{2,11},{3,12},{4,13},{5,14},{6,15},{16,25},{17,26},{1... | collective-permute-start | bytes 37748744 | tf_op jit(solution)/shard_map/ppermute | solution.py:17
  36.4 8.9 %collective-permute-start.3 = (bf16[24,256,256]{2,1,0:T(8,128)(2,1)}, bf16[24,256,256]{2,1,0:T(8,128)(2,1)}, u32[]{:S(2)}, u32[]{:S(2)}) collective-permute-start(bf16[24,256,256]{2,1,0:T(8,128)(2,1)} %slice_bitcast_fusion), channel_id=1, source_target_pairs={{0,8},{1,9},{2,10},{3,11},{4,12},{5,13},{6,14},{7,15},{16,24},{17,... | collective-permute-start | bytes 9437192 | tf_op jit(solution)/shard_map/ppermute | solution.py:17
  50.4 332.7 %all-gather.2 = bf16[256,3,6]{2,0,1:T(8,128)(2,1)S(1)} all-gather(bf16[16,3,6]{2,0,1:T(8,128)(2,1)S(1)} %dynamic-slice_select_fusion.2), channel_id=4, replica_groups=mesh['row'=8,'col'=16] {'col'}, dimensions={0}, use_global_device_ids=true | all-gather | bytes 9792 | tf_op jit(solution)/shard_map/all_gather | solution.py:11
  407.4 7.7 %mul.255 = bf16[2,48,96,256]{3,2,0,1:T(8,128)(2,1)} reshape(bf16[2,48,6,4,4,256]{5,4,3,2,0,1:T(4,128)(2,1)} %mul.254) | data formatting | bytes 9437184 | tf_op jit(solution)/shard_map/mul | solution.py:45
  419.8 6.8 mul.239
  437.3 13.5 %gather_fusion.4 = bf16[288,2,16,256]{3,2,1,0:T(8,128)(2,1)} fusion(bf16[2,48,16,256]{3,2,1,0:T(8,128)(2,1)S(1)} %constant_dynamic-slice_fusion.6, s32[1024]{0:T(1024)S(1)} %pad_clamp_fusion), kind=kCustom, calls=%fused_computation.4 | custom fusion | bytes 9438336 | tf_op jit(solution)/shard_map/jit(_take)/gather | solution.py:43
  458.6 6.2 convert_bitcast_fusion.1
  464.8 5.7 reshape.941
  470.5 20.4 %convolution_bitcast_fusion.1 = f32[3,24,6,4,4,4,4]{6,5,4,3,2,1,0:T(4,128)} fusion(bf16[3,6,4,256]{3,2,1,0:T(4,128)(2,1)} %get-tuple-element.18, bf16[3,24,6,4,4,256]{5,4,3,2,0,1:T(4,128)(2,1)S(1)} %reshape.941, bf16[3,24,6,4,256]{4,3,0,2,1:T(4,128)(2,1)} %get-tuple-element.10), kind=kOutput, calls=%fused_computation.13 | convolution fusion | flops 63700992 | bytes 4902912 | tf_op jit(solution)/shard_map/tqiach,tqivwh->tqivawc/dot_general | solution.py:57
  490.8 13.2 %copy.64 = f32[3,24,6,4,4,4,4]{1,6,5,4,3,2,0:T(4,128)S(1)} copy(f32[3,24,6,4,4,4,4]{6,5,4,3,2,1,0:T(4,128)} %convolution_bitcast_fusion.1) | data formatting | bytes 884736 | tf_op jit(solution)/shard_map/tqiach,tqivwh->tqivawc/transpose | solution.py:57
  509.9 5.8 multiply_reduce_fusion.2
  521.8 9.5 %convert_bitcast_fusion = bf16[2,48,96,256]{3,2,0,1:T(8,128)(2,1)} fusion(bf16[2,48,96,256]{3,2,0,1:T(8,128)(2,1)} %mul.255, bf16[2,48,256,256]{3,2,1,0:T(8,128)(2,1)} %collective-permute-done.4, bf16[3,48,256,256]{3,2,1,0:T(8,128)(2,1)} %param.8, pred[]{:T(512)S(6)} %ge.124, bf16[2,96,256]{2,1,0:T(8,128)(2,1)S(1)} %copy-done.14), kind=kOutput, calls=%fused_computation.34 | convolution fusion | flops 1222901760 | bytes 22118400 | tf_op jit(solution)/shard_map/tqmg,qgh->tqmh/dot_general | solution.py:50
  531.2 7.8 %reshape.943 = bf16[2,48,6,4,4,256]{5,4,3,2,0,1:T(4,128)(2,1)} reshape(bf16[2,48,96,256]{3,2,0,1:T(8,128)(2,1)} %convert_bitcast_fusion) | data formatting | bytes 9437184 | tf_op jit(solution)/shard_map/reshape | solution.py:56
  539.1 46.0 %convolution_bitcast_fusion = f32[2,48,6,4,4,4,4]{6,5,4,3,2,1,0:T(4,128)} fusion(bf16[2,6,4,256]{3,2,1,0:T(4,128)(2,1)S(1)} %copy-done.20, bf16[2,48,6,4,4,256]{5,4,3,2,0,1:T(4,128)(2,1)} %reshape.943, bf16[2,48,6,4,256]{4,3,0,2,1:T(4,128)(2,1)S(1)} %copy-done.4), kind=kOutput, calls=%fused_computation.12 | convolution fusion | flops 84934656 | bytes 6512640 | tf_op jit(solution)/shard_map/tqiach,tqivwh->tqivawc/dot_general | solution.py:57
  585.0 15.6 %copy.73 = f32[2,48,6,4,4,4,4]{1,6,5,4,3,2,0:T(4,128)S(1)} copy(f32[2,48,6,4,4,4,4]{6,5,4,3,2,1,0:T(4,128)} %convolution_bitcast_fusion) | data formatting | bytes 1179648 | tf_op jit(solution)/shard_map/tqiach,tqivwh->tqivawc/transpose | solution.py:57
  604.2 5.9 multiply_reduce_fusion.1
  612.4 8.2 %convert_bitcast_fusion.2 = bf16[1,48,96,256]{3,2,1,0:T(8,128)(2,1)} fusion(bf16[2,48,256,256]{3,2,1,0:T(8,128)(2,1)} %collective-permute-done.4, bf16[3,48,256,256]{3,2,1,0:T(8,128)(2,1)} %param.8, pred[]{:T(512)S(6)} %ge.124, bf16[48,96,256]{2,1,0:T(8,128)(2,1)S(1)} %copy-done.3, bf16[96,256]{1,0:T(8,128)(2,1)S(1)} %copy-done.15), kind=kOutput, calls=%fused_computation.68 | convolution fusion | flops 613023744 | bytes 17350656 | tf_op jit(solution)/shard_map/tqmg,qgh->tqmh/dot_general | solution.py:50
  620.7 4.1 reshape.1102
  624.8 13.0 %convolution_bitcast_fusion.2 = f32[1,48,6,4,4,4,4]{6,5,4,3,2,1,0:T(4,128)} fusion(bf16[48,6,4,4,256,1]{4,3,2,1,0,5:T(4,128)(2,1)S(1)} %reshape.1102, bf16[48,6,4,256]{3,2,1,0:T(4,128)(2,1)S(1)} %copy-done.7, bf16[6,4,256]{2,1,0:T(4,128)(2,1)S(1)} %copy-done.23), kind=kOutput, calls=%fused_computation.24 | convolution fusion | flops 42467328 | bytes 3256320 | tf_op jit(solution)/shard_map/tqiach,tqivwh->tqivawc/dot_general | solution.py:57
  637.8 8.2 %copy.80 = f32[1,48,6,4,4,4,4]{1,6,5,4,3,2,0:T(4,128)S(1)} copy(f32[1,48,6,4,4,4,4]{6,5,4,3,2,1,0:T(4,128)} %convolution_bitcast_fusion.2) | data formatting | bytes 589824 | tf_op jit(solution)/shard_map/tqiach,tqivwh->tqivawc/transpose | solution.py:57
  648.5 4.5 fusion.41
  656.2 53.0 %all-reduce = f32[16,3,6]{2,1,0:T(4,128)S(1)} all-reduce(f32[16,3,6]{2,1,0:T(4,128)S(1)} %copy.82), channel_id=5, replica_groups=mesh['row'=8,'col'=16] {'col'}, use_global_device_ids=true, to_apply=%region_2.3.clone | all-reduce | flops 288 | bytes 2304
  710.6 43.9 %all-reduce.1 = f32[16,3,48]{0,1,2:T(4,128)S(1)} all-reduce(f32[16,3,48]{0,1,2:T(4,128)S(1)} %copy.85), channel_id=6, replica_groups=mesh['row'=8,'col'=16] {'row'}, use_global_device_ids=true, to_apply=%region_4.5.clone | all-reduce | flops 2304 | bytes 18432
  (222 shorter events, 86.2 us)
Async XLA Ops:
  7.2 40.1 %copy-start = (s32[3,6,48]{2,1,0:T(8,128)S(1)}, s32[3,6,48]{2,1,0:T(8,128)}, u32[]{:S(2)}) copy-start(s32[3,6,48]{2,1,0:T(8,128)} %param.10) | copy-start | bytes 10372
  7.2 446.6 %all-gather.8.cloned.1.call-start = ((), (), s32[]{:S(2)}) async-start(), calls=%async_computation.1 | async-start | bytes 1253376 | tf_op jit(solution)/shard_map/all_gather | solution.py:11
  8.8 21.0 %copy-start.16 = (bf16[16,3,48]{2,0,1:T(8,128)(2,1)S(1)}, bf16[16,3,48]{2,0,1:T(8,128)(2,1)}, u32[]{:S(2)}) copy-start(bf16[16,3,48]{2,0,1:T(8,128)(2,1)} %param.11) | copy-start | bytes 13828
  8.8 498.4 %all-gather.6.cloned.1.call-start = ((), (), s32[]{:S(2)}) async-start(), calls=%async_computation | async-start | bytes 2506752 | tf_op jit(solution)/shard_map/all_gather | solution.py:11
  8.9 389.5 %collective-permute-start.2 = (bf16[3,48,8,256]{3,2,1,0:T(8,128)(2,1)}, bf16[3,48,8,256]{3,2,1,0:T(8,128)(2,1)S(1)}, u32[]{:S(2)}, u32[]{:S(2)}) collective-permute-start(bf16[3,48,8,256]{3,2,1,0:T(8,128)(2,1)} %param.6), channel_id=1, source_target_pairs={{8,0},{9,1},{10,2},{11,3},{12,4},{13,5},{14,6},{15,7},{24,16},{25,... | collective-permute-start | bytes 1769480 | tf_op jit(solution)/shard_map/ppermute | solution.py:17
  20.7 501.0 %collective-permute-start.4 = (bf16[2,48,256,256]{3,2,1,0:T(8,128)(2,1)}, bf16[2,48,256,256]{3,2,1,0:T(8,128)(2,1)}, u32[]{:S(2)}, u32[]{:S(2)}) collective-permute-start(bf16[2,48,256,256]{3,2,1,0:T(8,128)(2,1)} %slice.69), channel_id=1, source_target_pairs={{0,9},{1,10},{2,11},{3,12},{4,13},{5,14},{6,15},{16,25},{17,26},{1... | collective-permute-start | bytes 37748744 | tf_op jit(solution)/shard_map/ppermute | solution.py:17
  29.8 360.7 %collective-permute-start = (bf16[16,3,48]{2,0,1:T(8,128)(2,1)S(1)}, bf16[16,3,48]{2,0,1:T(8,128)(2,1)S(1)}, u32[]{:S(2)}, u32[]{:S(2)}) collective-permute-start(bf16[16,3,48]{2,0,1:T(8,128)(2,1)S(1)} %copy-done.16), channel_id=1, source_target_pairs={{8,0},{9,1},{10,2},{11,3},{12,4},{13,5},{14,6},{15,7},{24,16},{25,... | collective-permute-start | bytes 13832 | tf_op jit(solution)/shard_map/ppermute | solution.py:17
  31.1 401.9 %collective-permute-start.1 = (bf16[3,48,16,256]{3,2,1,0:T(8,128)(2,1)}, bf16[3,48,16,256]{3,2,1,0:T(8,128)(2,1)}, u32[]{:S(2)}, u32[]{:S(2)}) collective-permute-start(bf16[3,48,16,256]{3,2,1,0:T(8,128)(2,1)} %param.7), channel_id=1, source_target_pairs={{8,0},{9,1},{10,2},{11,3},{12,4},{13,5},{14,6},{15,7},{24,16},{25,... | collective-permute-start | bytes 3538952 | tf_op jit(solution)/shard_map/ppermute | solution.py:17
  36.4 352.2 %copy-start.32 = (u32[128]{0:T(128)S(1)}, u32[128]{0:T(128)}, u32[]{:S(2)}) copy-start(u32[128]{0:T(128)} %constant.315) | copy-start | bytes 1540
  36.4 352.9 %copy-start.31 = (u32[128]{0:T(128)S(1)}, u32[128]{0:T(128)}, u32[]{:S(2)}) copy-start(u32[128]{0:T(128)} %constant.311) | copy-start | bytes 1540
  36.4 422.2 %collective-permute-start.3 = (bf16[24,256,256]{2,1,0:T(8,128)(2,1)}, bf16[24,256,256]{2,1,0:T(8,128)(2,1)}, u32[]{:S(2)}, u32[]{:S(2)}) collective-permute-start(bf16[24,256,256]{2,1,0:T(8,128)(2,1)} %slice_bitcast_fusion), channel_id=1, source_target_pairs={{0,8},{1,9},{2,10},{3,11},{4,12},{5,13},{6,14},{7,15},{16,24},{17,... | collective-permute-start | bytes 9437192 | tf_op jit(solution)/shard_map/ppermute | solution.py:17
  49.6 340.9 %copy-start.17 = (s32[24,6]{0,1:T(8,128)}, s32[24,6]{0,1:T(8,128)S(1)}, u32[]{:S(2)}) copy-start(s32[24,6]{0,1:T(8,128)S(1)} %copy.58) | copy-start | bytes 1732
  384.4 6.2 copy-start.26
  385.9 14.5 %copy-start.9 = (pred[48,6]{1,0:T(8,128)(4,1)}, pred[48,6]{1,0:T(8,128)(4,1)S(1)}, u32[]{:S(2)}) copy-start(pred[48,6]{1,0:T(8,128)(4,1)S(1)} %copy.66) | copy-start | bytes 868
  419.8 8.6 %copy-start.10 = (pred[48,6]{1,0:T(8,128)(4,1)S(1)}, pred[48,6]{1,0:T(8,128)(4,1)}, u32[]{:S(2)}) copy-start(pred[48,6]{1,0:T(8,128)(4,1)} %copy-done.9) | copy-start | bytes 868
  531.2 7.8 %copy-start.4 = (bf16[2,48,6,4,256]{4,3,0,2,1:T(4,128)(2,1)S(1)}, bf16[2,48,6,4,256]{4,3,0,2,1:T(4,128)(2,1)}, u32[]{:S(2)}) copy-start(bf16[2,48,6,4,256]{4,3,0,2,1:T(4,128)(2,1)} %get-tuple-element.8) | copy-start | bytes 3538948
  531.2 7.8 %copy-start.20 = (bf16[2,6,4,256]{3,2,1,0:T(4,128)(2,1)S(1)}, bf16[2,6,4,256]{3,2,1,0:T(4,128)(2,1)}, u32[]{:S(2)}) copy-start(bf16[2,6,4,256]{3,2,1,0:T(4,128)(2,1)} %get-tuple-element.16) | copy-start | bytes 73732
  604.2 6.0 copy-start.19
  637.8 10.6 %copy-start.2 = (bf16[288,16,256]{2,1,0:T(8,128)(2,1)S(1)}, bf16[288,16,256]{2,1,0:T(8,128)(2,1)}, u32[]{:S(2)}) copy-start(bf16[288,16,256]{2,1,0:T(8,128)(2,1)} %gather_fusion.7) | copy-start | bytes 7077892
  637.8 10.6 %copy-start.11 = (pred[48,6]{1,0:T(8,128)(4,1)S(1)}, pred[48,6]{1,0:T(8,128)(4,1)}, u32[]{:S(2)}) copy-start(pred[48,6]{1,0:T(8,128)(4,1)} %copy-done.9) | copy-start | bytes 868
  637.8 10.6 %copy-start.12 = (f32[6,48,16]{2,1,0:T(8,128)S(1)}, f32[6,48,16]{2,1,0:T(8,128)}, u32[]{:S(2)}) copy-start(f32[6,48,16]{2,1,0:T(8,128)} %copy.147) | copy-start | bytes 55300
  637.8 10.6 %copy-start.29 = (pred[48,6]{0,1:T(8,128)(4,1)S(1)}, pred[48,6]{0,1:T(8,128)(4,1)}, u32[]{:S(2)}) copy-start(pred[48,6]{0,1:T(8,128)(4,1)} %get-tuple-element.27) | copy-start | bytes 868
  648.5 106.6 %copy-start.1 = (s32[3,6,48]{2,1,0:T(8,128)S(1)}, s32[3,6,48]{2,1,0:T(8,128)}, u32[]{:S(2)}) copy-start(s32[3,6,48]{2,1,0:T(8,128)} %param.10) | copy-start | bytes 10372
  654.7 55.8 %collective-permute-start.5 = (f32[16,3,48]{2,0,1:T(8,128)S(1)}, f32[16,3,48]{2,0,1:T(8,128)S(1)}, u32[]{:S(2)}, u32[]{:S(2)}) collective-permute-start(f32[16,3,48]{2,0,1:T(8,128)S(1)} %fusion.71), channel_id=1, source_target_pairs={{0,8},{1,9},{2,10},{3,11},{4,12},{5,13},{6,14},{7,15},{16,24},{17,... | collective-permute-start | bytes 27656 | tf_op jit(solution)/shard_map/ppermute | solution.py:17
  (17 other events, 69.4 us)
Sparse Core Ops, SparseCore 0:
  9.7 38.6 all-gather.7
  50.1 358.9 all-gather.5
